TPU v7x, 32 devices: a whole 2x2x4 slice. The times are simulated.
32 devices in a mesh: rep: 8 (over y, x, core), tp: 4 (over z).
Axes of the slice: x: 2, y: 2, z: 4, core: 2. Of those that a mesh axis runs over, the one named last changes fastest.
Arguments:
- tokens: bfloat16 [4096, 8192], P('rep', 'tp'), may hold values from -6 to 6
- query_weight: bfloat16 [8192, 4096], P(None, 'tp'), may hold values from -0.0625 to 0.0625
- key_value_weight: bfloat16 [8192, 1024], P('tp'), may hold values from -0.0625 to 0.0625
- adapter_down_tables: bfloat16 [32, 192, 8192], P('rep', None, 'tp'), may hold values from -0.0625 to 0.0625
- adapter_up_query: bfloat16 [32, 64, 4096], P('rep', None, 'tp'), may hold values from -0.75 to 0.75
- adapter_up_key_value: bfloat16 [32, 64, 1024], P('rep', None, 'tp'), may hold values from -0.75 to 0.75
- request_adapter: int32 [128], P('rep'), may hold values from 0 to 31, as said below
- request_token_length: int32 [128], P('rep'), may hold values from 8 to 32, as said below
- adapter_table_row: int32 [32], replicated, may hold values from 0 to 31, as said below
Outputs:
- attended: bfloat16 [4096, 4096], P('rep', 'tp')
Inputs may be any that keep to these rules, and one draw needn't show every extreme that they name: `request_adapter`: in each replica's block of 16 requests at most 4 have adapters whose table rows adapter_table_row lies in one index of rep's share (rows s with the same s // 4); in every draw one share gets exactly 4 from every replica. `adapter_table_row`: A permutation of the table rows. `request_token_length`: every replica has one request of exactly 32 tokens.
All inputs are finite; a program needn't handle non-finite values.
Results may differ from a plain program's by a relative error of at most 0.0098.
Values may be sent and summed in bfloat16 or wider, within the bound.
A program may use at most 192 MiB of HBM per device.

v0:
```python
import math
import jax
import jax.numpy as jnp
from jax import lax
from jax.sharding import PartitionSpec as P

HEAD_SIZE = 128
adapter_scale = 0.5
rope_theta = 500000.0


def rotary(values, positions):
    half_dim = values.shape[-1] // 2
    frequency = rope_theta ** (-(jnp.arange(half_dim, dtype=jnp.float32) * 2.0 / values.shape[-1]))
    angles = positions.astype(jnp.float32)[:, None] * frequency[None, :]
    cosine = jnp.cos(angles)[:, None, :]
    sine_part = jnp.sin(angles)[:, None, :]
    lower_half = values[..., :half_dim]
    upper_half = values[..., half_dim:]
    return jnp.concatenate(
        [
            lower_half * cosine - upper_half * sine_part,
            upper_half * cosine + lower_half * sine_part,
        ],
        axis=-1,
    )


def expand_slots(shrink, query_up_weight, key_value_up_weight, value_side):
    rank_size = query_up_weight.shape[2]
    query_change = jnp.einsum(
        "sinr,sirc->sinc",
        shrink[..., :rank_size],
        query_up_weight,
        preferred_element_type=jnp.float32,
    )
    pair_input = jnp.where(
        value_side, shrink[..., 2 * rank_size :], shrink[..., rank_size : 2 * rank_size]
    )
    key_value_update = jnp.einsum(
        "sinr,sirc->sinc", pair_input, key_value_up_weight, preferred_element_type=jnp.float32
    )
    return (adapter_scale * jnp.concatenate([query_change, key_value_update], axis=-1)).astype(
        jnp.bfloat16
    )


def shards(
    tokens,
    query_weight,
    key_value_weight,
    adapter_down_tables,
    adapter_up_query,
    adapter_up_key_value,
    request_adapter,
    request_token_length,
    adapter_table_row,
):
    replicas = lax.axis_size("rep")
    tp_count = lax.axis_size("tp")
    tp_here = lax.axis_index("tp")
    tok_rows = tokens.shape[0]
    feat_local = tokens.shape[1]
    query_cols = query_weight.shape[1]
    pair_total = key_value_weight.shape[1]
    portion_value = adapter_up_key_value.shape[2]
    local_table_rows = adapter_down_tables.shape[0]
    requests_here = request_adapter.shape[0]
    seq_len = tok_rows // requests_here
    capacity = max(1, 2 * requests_here // replicas)
    slot_count = replicas * capacity
    delta_cols = query_cols + portion_value
    value_side = tp_here >= tp_count // 2
    base_query = jnp.dot(
        lax.all_gather(tokens, "tp", axis=1, tiled=True),
        query_weight,
        preferred_element_type=jnp.float32,
    )
    base_pair = jnp.dot(tokens, key_value_weight, preferred_element_type=jnp.float32)
    id_match = (
        request_adapter[:, None] == jnp.arange(adapter_table_row.shape[0], dtype=jnp.int32)[None, :]
    )
    homes = jnp.sum(jnp.where(id_match, adapter_table_row[None, :], 0), axis=1)
    owners = homes // local_table_rows
    local_ids = homes % local_table_rows
    request_pos = jnp.arange(requests_here, dtype=jnp.int32)
    earlier = (owners[:, None] == owners[None, :]) & (request_pos[None, :] < request_pos[:, None])
    slot_ids = owners * capacity + jnp.sum(earlier.astype(jnp.int32), axis=1)
    placement = slot_ids[None, :] == jnp.arange(slot_count, dtype=jnp.int32)[:, None]
    place_matrix = placement.astype(jnp.bfloat16)
    send_rows = jnp.dot(
        place_matrix,
        tokens.reshape(requests_here, seq_len * feat_local),
        preferred_element_type=jnp.float32,
    )
    send_rows = send_rows.astype(jnp.bfloat16).reshape(replicas, capacity, seq_len, feat_local)
    slot_local = jnp.sum(jnp.where(placement, local_ids[None, :], 0), axis=1).reshape(
        replicas, capacity
    )
    needed_locally = lax.all_to_all(slot_local, "rep", split_axis=0, concat_axis=0, tiled=True)
    fetched_down, fetched_query, fetched_pair = (
        lax.all_to_all(
            jnp.take(adapter_down_tables, needed_locally, axis=0),
            "rep",
            split_axis=0,
            concat_axis=0,
            tiled=True,
        ),
        lax.all_to_all(
            jnp.take(adapter_up_query, needed_locally, axis=0),
            "rep",
            split_axis=0,
            concat_axis=0,
            tiled=True,
        ),
        lax.all_to_all(
            jnp.take(adapter_up_key_value, needed_locally, axis=0),
            "rep",
            split_axis=0,
            concat_axis=0,
            tiled=True,
        ),
    )
    partial_sum = jnp.einsum(
        "scnf,scrf->scnr", send_rows, fetched_down, preferred_element_type=jnp.float32
    )
    shrink = lax.psum(partial_sum, "tp").astype(jnp.bfloat16)
    returned = expand_slots(shrink, fetched_query, fetched_pair, value_side)
    delta = jnp.dot(
        place_matrix.T,
        returned.reshape(slot_count, seq_len * delta_cols),
        preferred_element_type=jnp.float32,
    )
    delta = delta.reshape(tok_rows, delta_cols)
    positions = jnp.arange(tok_rows, dtype=jnp.int32) % seq_len
    heads_here = query_cols // HEAD_SIZE
    query = rotary(
        (base_query + delta[:, :query_cols]).reshape(tok_rows, heads_here, HEAD_SIZE), positions
    ).astype(jnp.bfloat16)
    placed = lax.dynamic_update_slice_in_dim(
        jnp.zeros((tok_rows, pair_total), jnp.float32),
        delta[:, query_cols:],
        tp_here * portion_value,
        1,
    )
    pair_full = lax.psum(base_pair + placed, "tp")
    pair_raw = lax.optimization_barrier(pair_full.astype(jnp.bfloat16))
    kv_heads = pair_total // (2 * HEAD_SIZE)
    head_index = tp_here // (tp_count // kv_heads)
    keys_raw = lax.dynamic_slice_in_dim(pair_raw, head_index * HEAD_SIZE, HEAD_SIZE, 1)
    values = lax.dynamic_slice_in_dim(
        pair_raw, kv_heads * HEAD_SIZE + head_index * HEAD_SIZE, HEAD_SIZE, 1
    )
    keys = rotary(keys_raw.astype(jnp.float32).reshape(tok_rows, 1, HEAD_SIZE), positions).astype(
        jnp.bfloat16
    )
    query_blocks = query.reshape(requests_here, seq_len, heads_here, HEAD_SIZE)
    key_blocks = keys.reshape(requests_here, seq_len, HEAD_SIZE)
    value_blocks = values.reshape(requests_here, seq_len, HEAD_SIZE)
    scores = jnp.einsum(
        "rqhd,rpd->rhqp", query_blocks, key_blocks, preferred_element_type=jnp.float32
    ) / math.sqrt(HEAD_SIZE)
    slot_pos = jnp.arange(seq_len, dtype=jnp.int32)
    allowed = (slot_pos[None, None, :] <= slot_pos[None, :, None]) & (
        slot_pos[None, None, :] < request_token_length[:, None, None]
    )
    scores = jnp.where(allowed[:, None, :, :], scores, jnp.float32(-1e30))
    peak = jnp.max(scores, axis=-1, keepdims=True)
    weights = jnp.exp(scores - peak)
    probs = (weights / jnp.sum(weights, axis=-1, keepdims=True)).astype(jnp.bfloat16)
    mixed = jnp.einsum("rhqp,rpd->rqhd", probs, value_blocks, preferred_element_type=jnp.float32)
    live = slot_pos[None, :] < request_token_length[:, None]
    mixed = jnp.where(live[:, :, None, None], mixed, jnp.float32(0.0))
    return mixed.astype(jnp.bfloat16).reshape(tok_rows, query_cols)


def solution(mesh):
    placed = (
        P("rep", "tp"),
        P(None, "tp"),
        P("tp", None),
        P("rep", None, "tp"),
        P("rep", None, "tp"),
        P("rep", None, "tp"),
        P("rep"),
        P("rep"),
        P(),
    )
    return jax.shard_map(
        shards, mesh=mesh, in_specs=placed, out_specs=P("rep", "tp"), check_vma=False
    )
```

profile of v0, /device:TPU:0, one launch (start us, length us, event | category | flops | bytes accessed | tf_op | source)
XLA Modules:
  0.0 532.3 jit_solution(14135804955367768476)
XLA Ops:
  6.5 0.0 copy-start
  6.5 1.0 select_reduce_fusion.1
  7.6 0.2 convert_reduce_fusion
  7.7 0.1 select_reduce_fusion
  7.8 0.1 all_to_all.19
  7.9 9.6 %all_to_all.30 = s32[8,1,4]{2,1,0:T(1,128)S(1)} all-to-all(s32[8,1,4]{2,1,0:T(1,128)S(1)} %bitcast.83), channel_id=1, replica_groups=mesh['rep'=8,'tp'=4] {'rep'}, dimensions={0} | all-to-all | bytes 256 | tf_op jit(solution)/shard_map/all_to_all | solution.py:100
  17.5 0.1 copy.39
  17.6 0.1 copy.42
  17.7 0.1 reshape.322
  17.8 0.1 copy.40
  17.9 0.0 copy-done
  17.9 9.9 %gather_fusion = bf16[32,192,2048]{2,1,0:T(8,128)(2,1)} fusion(bf16[4,192,2048]{2,1,0:T(8,128)(2,1)S(1)} %copy-done, s32[1024]{0:T(1024)S(1)} %pad_clamp_fusion), kind=kCustom, calls=%fused_computation | custom fusion | bytes 50331776 | tf_op jit(solution)/shard_map/jit(_take)/gather | solution.py:103
  27.8 0.0 copy-done.4
  27.8 0.6 gather_fusion.2
  28.5 1.1 broadcast_select_fusion.2
  29.6 3.6 all-to-all-start.3
  33.2 21.2 %broadcast_select_fusion = bf16[8,4,192,2048]{3,2,1,0:T(8,128)(2,1)} fusion(bf16[8,4,192,2048]{3,2,1,0:T(8,128)(2,1)} %bitcast.69, pred[8,4]{1,0:T(8,128)(4,1)S(1)} %copy.40), kind=kLoop, calls=%fused_computation.5 | loop fusion | flops 12582912 | bytes 50331680 | tf_op jit(solution)/shard_map/jit(_take)/select_n | solution.py:103
  54.4 0.0 all-to-all-done.3
  54.4 1.0 copy-done.5
  55.3 6.4 %all-to-all-start.1 = ((bf16[8,4,192,2048]{3,2,1,0:T(8,128)(2,1)}), bf16[8,4,192,2048]{3,2,1,0:T(8,128)(2,1)}, u32[]{:S(2)}, u32[]{:S(2)}) async-start(bf16[8,4,192,2048]{3,2,1,0:T(8,128)(2,1)} %broadcast_select_fusion), calls=%async_computation.1 | async-start | bytes 50331648 | tf_op jit(solution)/shard_map/all_to_all | solution.py:102
  61.8 0.0 all-gather.2.cloned.1.call-start
  61.8 0.7 all-gather.2.cloned.1.call-update
  62.5 0.0 copy-start.10
  62.5 2.2 reshape.310
  64.8 0.0 copy-done.10
  64.8 0.1 iota_compare_fusion.6
  64.8 3.3 convolution_convert_fusion
  68.1 0.0 copy-done.2
  68.1 2.8 gather_fusion.1
  70.9 5.1 broadcast_select_fusion.1
  76.0 259.6 %all-to-all-done.1 = bf16[8,4,192,2048]{3,2,1,0:T(8,128)(2,1)} async-done(((bf16[8,4,192,2048]{3,2,1,0:T(8,128)(2,1)}), bf16[8,4,192,2048]{3,2,1,0:T(8,128)(2,1)}, u32[]{:S(2)}, u32[]{:S(2)}) %all-to-all-start.1) | async-done | bytes 25165856 | tf_op jit(solution)/shard_map/all_to_all | solution.py:102
  335.6 4.8 all-to-all-start.2
  340.4 0.0 copy-start.3
  340.4 6.6 %copy.52 = bf16[4,8,32,2048]{3,2,1,0:T(8,128)(2,1)} copy(bf16[4,8,32,2048]{3,1,2,0:T(8,128)(2,1)} %bitcast.71) | data formatting | bytes 8388608
  347.0 0.8 broadcast_and_fusion
  347.8 1.7 multiply_cosine_fusion
  349.5 5.8 %fusion.48 = f32[512,1024]{1,0:T(8,128)} fusion(bf16[512,2048]{1,0:T(8,128)(2,1)S(1)} %copy-done.3, bf16[2048,1024]{1,0:T(8,128)(2,1)} %param.11), kind=kOutput, calls=%fused_computation.86 | convolution fusion | flops 2147483648 | bytes 8388608 | tf_op jit(solution)/shard_map/dot_general | solution.py:79
  355.4 13.4 %fusion.49 = f32[8,4,32,192]{3,2,1,0:T(8,128)S(1)} fusion(bf16[8,4,32,2048]{3,2,1,0:T(8,128)(2,1)} %bitcast.73, bf16[8,4,192,2048]{3,2,1,0:T(8,128)(2,1)} %all-to-all-done.1), kind=kOutput, calls=%fused_computation.87 | convolution fusion | flops 805306368 | bytes 30146560 | tf_op jit(solution)/shard_map/scnf,scrf->scnr/dot_general | solution.py:124
  368.8 43.8 %all-reduce.2 = bf16[8,4,32,192]{3,2,1,0:T(8,128)(2,1)S(1)} all-reduce(f32[8,4,32,192]{3,2,1,0:T(8,128)S(1)} %fusion.49), channel_id=1, replica_groups=mesh['rep'=8,'tp'=4] {'tp'}, use_global_device_ids=true, to_apply=%region_3.4 | all-reduce | flops 196608 | bytes 1179648 | tf_op jit(solution)/shard_map/psum | solution.py:127
  412.7 0.4 fusion.21
  413.0 0.0 all-to-all-done.2
  413.0 2.9 fusion.23
  415.9 0.7 fusion.1
  416.6 1.4 copy.53
  418.1 2.1 fusion.32
  420.1 1.9 reshape.312
  422.1 2.0 fusion.12
  424.0 72.7 %all-reduce.3 = bf16[512,1024]{1,0:T(8,128)(2,1)} all-reduce(f32[512,1024]{1,0:T(8,128)} %fusion.12), channel_id=1, replica_groups=mesh['rep'=8,'tp'=4] {'tp'}, use_global_device_ids=true, to_apply=%region_4.5 | all-reduce | flops 524288 | bytes 3145728 | tf_op jit(solution)/shard_map/psum | solution.py:146
  496.7 1.0 bitcast_convert_fusion
  497.7 1.9 fusion.18
  499.6 14.4 %fusion.2 = f32[64,8,8,128]{3,1,2,0:T(8,128)S(1)} fusion(f32[512,1280]{1,0:T(8,128)S(1)} %reshape.312, bf16[512,8192]{1,0:T(8,128)(2,1)} %all-gather.2.cloned.1.call-done, bf16[8192,1024]{1,0:T(8,128)(2,1)} %param.10), kind=kOutput, calls=%fused_computation.10 | convolution fusion | flops 8590458880 | bytes 29360128 | tf_op jit(solution)/shard_map/dot_general | solution.py:74
  514.0 0.5 copy.54
  514.4 0.5 copy-done.7
  514.9 0.8 subtract_convert_fusion
  515.7 0.0 copy-start.8
  515.7 0.2 copy.45
  516.0 0.2 copy.46
  516.3 0.4 copy-done.8
  516.6 0.1 copy-done.9
  516.7 4.7 fusion.45
  521.4 2.3 fusion.4
  523.7 0.5 copy.48
  524.2 1.2 copy.57
  525.4 0.0 copy-done.1
  (18 shorter events, 0.1 us)
Async XLA Ops:
  6.5 11.4 %copy-start = (bf16[4,192,2048]{2,1,0:T(8,128)(2,1)S(1)}, bf16[4,192,2048]{2,1,0:T(8,128)(2,1)}, u32[]{:S(2)}) copy-start(bf16[4,192,2048]{2,1,0:T(8,128)(2,1)} %param.12) | copy-start | bytes 9437188
  17.9 9.9 %copy-start.4 = (bf16[4,64,256]{2,1,0:T(8,128)(2,1)S(1)}, bf16[4,64,256]{2,1,0:T(8,128)(2,1)}, u32[]{:S(2)}) copy-start(bf16[4,64,256]{2,1,0:T(8,128)(2,1)} %param.14) | copy-start | bytes 393220
  29.6 24.8 %all-to-all-start.3 = ((bf16[8,4,64,256]{3,2,1,0:T(8,128)(2,1)}), bf16[8,4,64,256]{3,2,1,0:T(8,128)(2,1)S(1)}, u32[]{:S(2)}, u32[]{:S(2)}) async-start(bf16[8,4,64,256]{3,2,1,0:T(8,128)(2,1)} %broadcast_select_fusion.2), calls=%async_computation.3 | async-start | bytes 2097152 | tf_op jit(solution)/shard_map/all_to_all | solution.py:116
  54.4 1.0 copy-start.5
  55.3 280.3 %all-to-all-start.1 = ((bf16[8,4,192,2048]{3,2,1,0:T(8,128)(2,1)}), bf16[8,4,192,2048]{3,2,1,0:T(8,128)(2,1)}, u32[]{:S(2)}, u32[]{:S(2)}) async-start(bf16[8,4,192,2048]{3,2,1,0:T(8,128)(2,1)} %broadcast_select_fusion), calls=%async_computation.1 | async-start | bytes 50331648 | tf_op jit(solution)/shard_map/all_to_all | solution.py:102
  61.8 437.8 %all-gather.2.cloned.1.call-start = ((), (), s32[]{:S(2)}) async-start(), calls=%async_computation.4 | async-start | bytes 10485760 | tf_op jit(solution)/shard_map/all_gather | solution.py:75
  62.5 2.3 copy-start.10
  64.8 3.3 copy-start.2
  335.6 77.4 %all-to-all-start.2 = ((bf16[8,4,64,1024]{3,2,1,0:T(8,128)(2,1)}), bf16[8,4,64,1024]{3,2,1,0:T(8,128)(2,1)}, u32[]{:S(2)}, u32[]{:S(2)}) async-start(bf16[8,4,64,1024]{3,2,1,0:T(8,128)(2,1)} %broadcast_select_fusion.1), calls=%async_computation.2 | async-start | bytes 8388608 | tf_op jit(solution)/shard_map/all_to_all | solution.py:109
  340.4 9.1 %copy-start.3 = (bf16[512,2048]{1,0:T(8,128)(2,1)S(1)}, bf16[512,2048]{1,0:T(8,128)(2,1)}, u32[]{:S(2)}) copy-start(bf16[512,2048]{1,0:T(8,128)(2,1)} %param.9) | copy-start | bytes 6291460
  355.4 57.3 %copy-start.6 = (bf16[8,4,64,256]{3,2,1,0:T(8,128)(2,1)S(1)}, bf16[8,4,64,256]{3,2,1,0:T(8,128)(2,1)}, u32[]{:S(2)}) copy-start(bf16[8,4,64,256]{3,2,1,0:T(8,128)(2,1)} %copy-done.5) | copy-start | bytes 3145732
  513.9 1.0 copy-start.7
  515.7 0.9 copy-start.8
  515.7 1.0 copy-start.9
  521.4 4.0 copy-start.1
Sparse Core Ops, SparseCore 0:
  64.2 151.2 all-gather.1
where the time goes:
time: 533 us; the launch traced here: 532 us
  waiting for transfers between devices  260 us (49%)
  blocking collectives  126 us (24%)
  matrix products  49.3 us (9%)
  other arithmetic  37.6 us (7%)
  local copies, waits for them, and re-layouts  30.5 us (6%)
  starting transfers between devices  14.8 us (3%)
  between operations  13.6 us (3%)
    all_to_all x1, waiting for transfers between devices, shards(): lax.all_to_all(jnp.take(adapter_down_tables, needed_locally, axis=0), 're...  260 us
    psum x1, blocking collectives, shards(): pair_full = lax.psum(base_pair + placed, 'tp')  72.7 us
    psum x1, blocking collectives, shards(): shrink = lax.psum(partial_sum, 'tp').astype(jnp.bfloat16)  43.8 us
    select_n x2, other arithmetic, shards(): jnp.take(adapter_down_tables, needed_locally, axis=0)  21.2 us
    dot_general x1, matrix products, shards(): jnp.dot(lax.all_gather(tokens, 'tp', axis=1, tiled=True), query_weight, p...  14.4 us
    dot_general x1, matrix products, shards(): jnp.einsum('scnf,scrf->scnr', send_rows, fetched_down, preferred_element_...  13.4 us
    unnamed x26, local copies, waits for them, and re-layouts  11.7 us
  transfers between devices with their start and end apart: 4, of which 1 were waited for; matrix products, arithmetic and copies ran while one was open for 15% of the time, Pallas kernels for 0%

commit v1 on v0

--- a/solution.py
+++ b/solution.py
@@ -124,7 +124,7 @@
     partial_sum = jnp.einsum(
         "scnf,scrf->scnr", send_rows, fetched_down, preferred_element_type=jnp.float32
     )
-    shrink = lax.psum(partial_sum, "tp").astype(jnp.bfloat16)
+    shrink = jnp.sum(lax.all_gather(partial_sum, "tp"), axis=0).astype(jnp.bfloat16)
     returned = expand_slots(shrink, fetched_query, fetched_pair, value_side)
     delta = jnp.dot(
         place_matrix.T,

time: 533 us -> 675 us (1.27)
  waiting for transfers between devices: 260 us -> 372 us
  blocking collectives: 126 us -> 157 us
    psum x1, blocking collectives: 72.7 us -> 147 us  [shards(): pair_full = lax.psum(base_pair + placed, 'tp')]
    all_gather x1, waiting for transfers between devices: 0.01 us -> 52.3 us  [shards(): lax.all_gather(tokens, 'tp', axis=1, tiled=True)]
    all_gather x0 -> x1, waiting for transfers between devices: none -> 45.6 us  [shards(): lax.all_gather(partial_sum, 'tp')]
    psum x1 -> x0, blocking collectives: 43.8 us -> none  [shards(): shrink = lax.psum(partial_sum, 'tp').astype(jnp.bfloat16)]
    all_to_all x1, waiting for transfers between devices: 0.01 us -> 7.81 us  [shards(): lax.all_to_all(jnp.take(adapter_up_key_value, needed_locally, axis=0), 'r...]
  transfers between devices with their start and end apart: 4 -> 5, of which waited for: 1 -> 4; matrix products, arithmetic and copies ran while one was open for 15% -> 6% of each run, Pallas kernels for 0% -> 0%
where the time goes in v1:
time: 675 us; the launch traced here: 674 us
  waiting for transfers between devices  372 us (55%)
  blocking collectives  157 us (23%)
  matrix products  48.4 us (7%)
  other arithmetic  40.1 us (6%)
  local copies, waits for them, and re-layouts  27.5 us (4%)
  starting transfers between devices  14.8 us (2%)
  between operations  13.6 us (2%)
    all_to_all x1, waiting for transfers between devices, shards(): lax.all_to_all(jnp.take(adapter_down_tables, needed_locally, axis=0), 're...  266 us
    psum x1, blocking collectives, shards(): pair_full = lax.psum(base_pair + placed, 'tp')  147 us
    all_gather x1, waiting for transfers between devices, shards(): lax.all_gather(tokens, 'tp', axis=1, tiled=True)  52.3 us
    all_gather x1, waiting for transfers between devices, shards(): lax.all_gather(partial_sum, 'tp')  45.6 us
    select_n x2, other arithmetic, shards(): jnp.take(adapter_down_tables, needed_locally, axis=0)  21.2 us
    dot_general x1, matrix products, shards(): jnp.einsum('scnf,scrf->scnr', send_rows, fetched_down, preferred_element_...  14.4 us
    dot_general x1, matrix products, shards(): jnp.dot(lax.all_gather(tokens, 'tp', axis=1, tiled=True), query_weight, p...  14.4 us
  transfers between devices with their start and end apart: 5, of which 4 were waited for; matrix products, arithmetic and copies ran while one was open for 6% of the time, Pallas kernels for 0%

profile of v1, /device:TPU:0, one launch (start us, length us, event | category | flops | bytes accessed | tf_op | source)
XLA Modules:
  0.0 673.7 jit_solution(2643766776227555749)
XLA Ops:
  6.5 0.0 copy-start
  6.5 1.0 select_reduce_fusion.1
  7.6 0.2 convert_reduce_fusion
  7.7 0.1 select_reduce_fusion
  7.8 0.1 all_to_all.19
  7.9 9.6 %all_to_all.30 = s32[8,1,4]{2,1,0:T(1,128)S(1)} all-to-all(s32[8,1,4]{2,1,0:T(1,128)S(1)} %bitcast.85), channel_id=1, replica_groups=mesh['rep'=8,'tp'=4] {'rep'}, dimensions={0} | all-to-all | bytes 256 | tf_op jit(solution)/shard_map/all_to_all | solution.py:100
  17.5 0.1 copy.39
  17.6 0.1 copy.42
  17.7 0.1 reshape.322
  17.8 0.1 copy.40
  17.9 0.0 copy-done
  17.9 9.9 %gather_fusion = bf16[32,192,2048]{2,1,0:T(8,128)(2,1)} fusion(bf16[4,192,2048]{2,1,0:T(8,128)(2,1)S(1)} %copy-done, s32[1024]{0:T(1024)S(1)} %pad_clamp_fusion), kind=kCustom, calls=%fused_computation | custom fusion | bytes 50331776 | tf_op jit(solution)/shard_map/jit(_take)/gather | solution.py:103
  27.8 21.2 %broadcast_select_fusion = bf16[8,4,192,2048]{3,2,1,0:T(8,128)(2,1)} fusion(bf16[8,4,192,2048]{3,2,1,0:T(8,128)(2,1)} %bitcast.70, pred[8,4]{1,0:T(8,128)(4,1)S(1)} %copy.40), kind=kLoop, calls=%fused_computation.5 | loop fusion | flops 12582912 | bytes 50331680 | tf_op jit(solution)/shard_map/jit(_take)/select_n | solution.py:103
  49.0 6.4 all-to-all-start.1
  55.5 0.0 all-gather.6.cloned.1.call-start
  55.5 2.2 reshape.310
  57.7 1.3 convolution_convert_fusion
  59.1 4.3 copy.52
  63.4 265.9 %all-to-all-done.1 = bf16[8,4,192,2048]{3,2,1,0:T(8,128)(2,1)} async-done(((bf16[8,4,192,2048]{3,2,1,0:T(8,128)(2,1)}), bf16[8,4,192,2048]{3,2,1,0:T(8,128)(2,1)}, u32[]{:S(2)}, u32[]{:S(2)}) %all-to-all-start.1) | async-done | bytes 25165856 | tf_op jit(solution)/shard_map/all_to_all | solution.py:102
  329.3 14.4 %fusion.49 = f32[8,4,32,192]{3,2,1,0:T(8,128)} fusion(bf16[8,4,32,2048]{3,2,1,0:T(8,128)(2,1)} %bitcast.74, bf16[8,4,192,2048]{3,2,1,0:T(8,128)(2,1)} %all-to-all-done.1), kind=kOutput, calls=%fused_computation.87 | convolution fusion | flops 805306368 | bytes 30146560 | tf_op jit(solution)/shard_map/scnf,scrf->scnr/dot_general | solution.py:124
  343.7 0.0 all-gather.6.cloned.1.call-update
  343.8 0.0 all-gather.4.cloned.1.call-start
  343.8 0.7 all-gather.4.cloned.1.call-update
  344.5 0.1 copy-done.4
  344.6 0.6 gather_fusion.2
  345.3 0.0 copy-start.2
  345.3 1.1 broadcast_select_fusion.2
  346.4 3.6 all-to-all-start.3
  350.0 0.0 copy-done.2
  350.0 2.8 gather_fusion.1
  352.7 4.8 broadcast_select_fusion.1
  357.5 7.8 %all-to-all-done.3 = bf16[8,4,64,256]{3,2,1,0:T(8,128)(2,1)S(1)} async-done(((bf16[8,4,64,256]{3,2,1,0:T(8,128)(2,1)}), bf16[8,4,64,256]{3,2,1,0:T(8,128)(2,1)S(1)}, u32[]{:S(2)}, u32[]{:S(2)}) %all-to-all-start.3) | async-done | bytes 1048608 | tf_op jit(solution)/shard_map/all_to_all | solution.py:116
  365.3 4.7 all-to-all-start.2
  370.1 0.1 iota_compare_fusion.6
  370.2 0.8 broadcast_and_fusion
  370.9 1.7 multiply_cosine_fusion
  372.7 5.8 fusion.48
  378.5 45.6 %all-gather.6.cloned.1.call-done = f32[32,4,32,192]{3,2,1,0:T(8,128)} async-done(((f32[8,4,32,192]{3,2,1,0:T(8,128)}), f32[32,4,32,192]{3,2,1,0:T(8,128)}) %all-gather.6.cloned.1.call-update) | async-done | bytes 3145744 | tf_op jit(solution)/shard_map/all_gather | solution.py:127
  424.1 2.8 reduce_sum.48
  426.9 0.4 fusion.21
  427.2 0.0 all-to-all-done.2
  427.2 2.9 fusion.23
  430.1 0.7 fusion.1
  430.8 1.4 copy.53
  432.3 2.1 fusion.32
  434.4 2.1 reshape.312
  436.5 2.0 fusion.12
  438.5 147.3 %all-reduce.1 = bf16[512,1024]{1,0:T(8,128)(2,1)} all-reduce(f32[512,1024]{1,0:T(8,128)} %fusion.12), channel_id=1, replica_groups=mesh['rep'=8,'tp'=4] {'tp'}, use_global_device_ids=true, to_apply=%region_4.5 | all-reduce | flops 524288 | bytes 3145728 | tf_op jit(solution)/shard_map/psum | solution.py:146
  585.8 1.0 bitcast_convert_fusion
  586.8 1.9 fusion.18
  588.7 52.3 %all-gather.4.cloned.1.call-done = bf16[512,8192]{1,0:T(8,128)(2,1)} async-done(((bf16[512,2048]{1,0:T(8,128)(2,1)}), bf16[512,8192]{1,0:T(8,128)(2,1)}) %all-gather.4.cloned.1.call-update) | async-done | bytes 8388624 | tf_op jit(solution)/shard_map/all_gather | solution.py:75
  641.0 14.4 %fusion.2 = f32[64,8,8,128]{3,1,2,0:T(8,128)S(1)} fusion(f32[512,1280]{1,0:T(8,128)S(1)} %reshape.312, bf16[512,8192]{1,0:T(8,128)(2,1)} %all-gather.4.cloned.1.call-done, bf16[8192,1024]{1,0:T(8,128)(2,1)} %param.10), kind=kOutput, calls=%fused_computation.10 | convolution fusion | flops 8590458880 | bytes 29360128 | tf_op jit(solution)/shard_map/dot_general | solution.py:74
  655.3 0.5 copy.54
  655.8 0.5 copy-done.5
  656.3 0.8 subtract_convert_fusion
  657.1 0.0 copy-start.6
  657.1 0.2 copy.45
  657.4 0.2 copy.46
  657.6 0.4 copy-done.6
  658.0 0.1 copy-done.7
  658.1 4.7 fusion.45
  662.8 2.3 fusion.4
  665.1 0.5 copy.48
  665.6 1.2 copy.57
  (17 shorter events, 0.1 us)
Async XLA Ops:
  6.5 11.4 %copy-start = (bf16[4,192,2048]{2,1,0:T(8,128)(2,1)S(1)}, bf16[4,192,2048]{2,1,0:T(8,128)(2,1)}, u32[]{:S(2)}) copy-start(bf16[4,192,2048]{2,1,0:T(8,128)(2,1)} %param.12) | copy-start | bytes 9437188
  49.0 280.3 %all-to-all-start.1 = ((bf16[8,4,192,2048]{3,2,1,0:T(8,128)(2,1)}), bf16[8,4,192,2048]{3,2,1,0:T(8,128)(2,1)}, u32[]{:S(2)}, u32[]{:S(2)}) async-start(bf16[8,4,192,2048]{3,2,1,0:T(8,128)(2,1)} %broadcast_select_fusion), calls=%async_computation.1 | async-start | bytes 50331648 | tf_op jit(solution)/shard_map/all_to_all | solution.py:102
  55.5 368.6 %all-gather.6.cloned.1.call-start = ((), (), s32[]{:S(2)}) async-start(), calls=%async_computation.5 | async-start | bytes 5242880 | tf_op jit(solution)/shard_map/all_gather | solution.py:127
  343.7 0.9 copy-start.4
  343.8 297.2 %all-gather.4.cloned.1.call-start = ((), (), s32[]{:S(2)}) async-start(), calls=%async_computation.4 | async-start | bytes 10485760 | tf_op jit(solution)/shard_map/all_gather | solution.py:75
  345.3 4.7 copy-start.2
  346.4 18.9 %all-to-all-start.3 = ((bf16[8,4,64,256]{3,2,1,0:T(8,128)(2,1)}), bf16[8,4,64,256]{3,2,1,0:T(8,128)(2,1)S(1)}, u32[]{:S(2)}, u32[]{:S(2)}) async-start(bf16[8,4,64,256]{3,2,1,0:T(8,128)(2,1)} %broadcast_select_fusion.2), calls=%async_computation.3 | async-start | bytes 2097152 | tf_op jit(solution)/shard_map/all_to_all | solution.py:116
  357.5 12.6 %copy-start.8 = (s32[16]{0:T(128)S(1)}, s32[16]{0:T(128)}, u32[]{:S(2)}) copy-start(s32[16]{0:T(128)} %param.16) | copy-start | bytes 196
  357.5 15.2 %copy-start.3 = (bf16[512,2048]{1,0:T(8,128)(2,1)S(1)}, bf16[512,2048]{1,0:T(8,128)(2,1)}, u32[]{:S(2)}) copy-start(bf16[512,2048]{1,0:T(8,128)(2,1)} %param.9) | copy-start | bytes 6291460
  365.3 61.9 %all-to-all-start.2 = ((bf16[8,4,64,1024]{3,2,1,0:T(8,128)(2,1)}), bf16[8,4,64,1024]{3,2,1,0:T(8,128)(2,1)}, u32[]{:S(2)}, u32[]{:S(2)}) async-start(bf16[8,4,64,1024]{3,2,1,0:T(8,128)(2,1)} %broadcast_select_fusion.1), calls=%async_computation.2 | async-start | bytes 8388608 | tf_op jit(solution)/shard_map/all_to_all | solution.py:109
  655.3 1.0 copy-start.5
  657.1 0.9 copy-start.6
  657.1 1.0 copy-start.7
  662.8 4.0 copy-start.1
Sparse Core Ops, SparseCore 0:
  343.9 80.1 all-gather.5
  425.6 215.2 all-gather.3
